TPU v7x, 512 devices: a whole 4x8x8 slice. The times are simulated.
512 devices in a mesh: dp: 64 (over z, y_hi, core), cls: 8 (over x, y_lo).
Axes of the slice: x: 4, y: 8 (y_hi: 4, y_lo: 2; y = y_hi * 2 + y_lo), z: 8, core: 2. Of those that a mesh axis runs over, the one named last changes fastest.
Arguments:
- features: bfloat16 [32768, 12544], P('dp', 'cls'), may hold values from -6 to 6
- fc_weight: bfloat16 [12544, 512], P('cls'), may hold values from -0.0546875 to 0.0546875
- class_weight: bfloat16 [4096, 512], P('cls'), may hold values from -0.29882812 to 0.29882812
- labels: int32 [32768], P('dp'), may hold values from 0 to 4095
Outputs:
- fc_grad: bfloat16 [12544, 512], P('cls')
- class_grad: bfloat16 [4096, 512], P('cls')
All inputs are finite; a program needn't handle non-finite values.
Results may differ from a plain program's by a relative error of at most 0.024.
Values may be sent and summed in bfloat16 or wider, within the bound.
No kernel may reach another device: no remote copies, remote signals or barrier semaphores. Data moves between devices by JAX's collectives and lax.ppermute only.
A program may use at most 64 MiB of HBM per device.

v0:
```python
import math
import jax
import jax.numpy as jnp
from jax import lax
from jax.sharding import PartitionSpec as P

SCALE = 64.0
MARGIN = 0.5
SOFTEN = 0.01
EPSILON = 1e-06


def margin_terms(cosine, is_target):
    sine = jnp.sqrt(1.0 + SOFTEN - cosine * cosine)
    shifted = cosine * math.cos(MARGIN) - sine * math.sin(MARGIN)
    powers = jnp.exp(SCALE * jnp.where(is_target, shifted, cosine))
    slopes = SCALE * jnp.where(is_target, math.cos(MARGIN) + math.sin(MARGIN) * cosine / sine, 1.0)
    return (powers, slopes)


def softmax_grad(powers, totals, slopes, is_target, loss_weight):
    onehot = is_target.astype(jnp.float32)
    return ((powers / totals[:, None] - onehot) * loss_weight * slopes).astype(jnp.bfloat16)


def shards(features, fc_weight, class_weight, labels):
    rows_group = features.shape[0]
    class_count = class_weight.shape[0]
    loss_weight = 1.0 / math.sqrt(rows_group * lax.axis_size("dp"))
    position = lax.axis_index("cls")
    rows_block = features
    raw_embed = lax.psum_scatter(
        jnp.dot(rows_block, fc_weight, preferred_element_type=jnp.float32).astype(jnp.bfloat16),
        "cls",
        scatter_dimension=0,
        tiled=True,
    ).astype(jnp.float32)
    embed_norm = jnp.sqrt(jnp.sum(raw_embed * raw_embed, axis=1, keepdims=True) + EPSILON)
    unit_f = raw_embed / embed_norm
    unit_embed = unit_f.astype(jnp.bfloat16)
    class_f = class_weight.astype(jnp.float32)
    class_norm = jnp.sqrt(jnp.sum(class_f * class_f, axis=1, keepdims=True) + EPSILON)
    class_unit_f = class_f / class_norm
    class_unit = class_unit_f.astype(jnp.bfloat16)
    faces_all = lax.all_gather(unit_embed, "cls", axis=0, tiled=True)
    cosine = lax.dot_general(
        faces_all, class_unit, (((1,), (1,)), ((), ())), preferred_element_type=jnp.float32
    )
    columns = position * class_count + lax.broadcasted_iota(jnp.int32, cosine.shape, 1)
    is_target = columns == labels[:, None]
    powers, slopes = margin_terms(cosine, is_target)
    totals = lax.psum(jnp.sum(powers, axis=1), "cls")
    cos_grad = softmax_grad(powers, totals, slopes, is_target, loss_weight)
    rows_block = cos_grad
    unit_grad = lax.psum_scatter(
        jnp.dot(rows_block, class_unit, preferred_element_type=jnp.float32).astype(jnp.bfloat16),
        "cls",
        scatter_dimension=0,
        tiled=True,
    ).astype(jnp.float32)
    class_part = lax.dot_general(
        cos_grad, faces_all, (((0,), (0,)), ((), ())), preferred_element_type=jnp.float32
    )
    raw_grad = (
        (unit_grad - unit_f * jnp.sum(unit_f * unit_grad, axis=1, keepdims=True)) / embed_norm
    ).astype(jnp.bfloat16)
    rows_block = features
    fc_part = lax.dot_general(
        rows_block,
        lax.all_gather(raw_grad, "cls", axis=0, tiled=True),
        (((0,), (0,)), ((), ())),
        preferred_element_type=jnp.float32,
    )
    fc_total, class_total = lax.psum((fc_part, class_part), "dp")
    fc_out = fc_total.astype(jnp.bfloat16)
    class_grad = (
        class_total - class_unit_f * jnp.sum(class_unit_f * class_total, axis=1, keepdims=True)
    ) / class_norm
    return (fc_out, class_grad.astype(jnp.bfloat16))


def solution(mesh):
    placed = (P("dp", "cls"), P("cls", None), P("cls", None), P("dp"))
    return jax.shard_map(
        shards,
        mesh=mesh,
        in_specs=placed,
        out_specs=(P("cls", None), P("cls", None)),
        check_vma=False,
    )
```

profile of v0, /device:TPU:4, one launch (start us, length us, event | category | flops | bytes accessed | tf_op | source)
XLA Modules:
  0.0 728.8 jit_solution(15242433414679928124)
XLA Ops:
  7.2 0.0 copy-start
  7.2 0.0 copy-start.1
  7.2 0.0 reduce-scatter.3.cloned.1.call-start
  7.2 1.4 copy-done
  8.6 3.4 convolution_convert_fusion.1
  11.9 0.0 copy-start.4
  11.9 0.0 reduce-scatter.3.cloned.1.call-update
  12.0 0.0 reduce-scatter.5.cloned.1.call-start
  12.0 0.0 copy-done.1
  12.0 0.2 fusion
  12.2 44.5 %reduce-scatter.3.cloned.1.call-done = bf16[64,512]{1,0:T(8,128)(2,1)} async-done(((bf16[512,512]{1,0:T(8,128)(2,1)}), bf16[64,512]{1,0:T(8,128)(2,1)}) %reduce-scatter.3.cloned.1.call-update) | async-done | bytes 65552 | tf_op jit(solution)/shard_map/reduce_scatter | solution.py:32
  56.8 1.0 fusion.12
  57.7 0.9 fusion.16
  58.7 30.1 %all_gather.6 = bf16[512,512]{1,0:T(8,128)(2,1)S(1)} all-gather(bf16[64,512]{1,0:T(8,128)(2,1)S(1)} %fusion.16), channel_id=1, replica_groups=mesh['dp'=64,'cls'=8] {'cls'}, dimensions={0}, use_global_device_ids=true | all-gather | bytes 589824 | tf_op jit(solution)/shard_map/all_gather | solution.py:45
  88.7 0.0 copy-done.4
  88.7 1.9 fusion.8
  90.6 16.5 %psum.21 = f32[512]{0:T(512)S(1)} all-reduce(f32[512]{0:T(512)S(1)} %get-tuple-element.2), channel_id=1, replica_groups=mesh['dp'=64,'cls'=8] {'cls'}, use_global_device_ids=true, to_apply=%region_4.5 | all-reduce | flops 512 | bytes 4096 | tf_op jit(solution)/shard_map/psum | solution.py:52
  107.1 2.2 fusion.6
  109.3 1.3 convolution_convert_fusion
  110.6 0.0 reduce-scatter.5.cloned.1.call-update
  110.7 0.0 copy-start.3
  110.7 0.0 all-reduce.3.cloned.1.call-start
  110.7 1.4 fusion.17
  112.1 0.0 all-reduce.3.cloned.1.call-update
  112.2 41.1 %reduce-scatter.5.cloned.1.call-done = bf16[64,512]{1,0:T(8,128)(2,1)} async-done(((bf16[512,512]{1,0:T(8,128)(2,1)}), bf16[64,512]{1,0:T(8,128)(2,1)}) %reduce-scatter.5.cloned.1.call-update) | async-done | bytes 65552 | tf_op jit(solution)/shard_map/reduce_scatter | solution.py:55
  153.3 0.0 copy-done.3
  153.3 1.0 fusion.13
  154.3 0.9 fusion.15
  155.3 30.2 %all_gather.7 = bf16[512,512]{1,0:T(8,128)(2,1)S(1)} all-gather(bf16[64,512]{1,0:T(8,128)(2,1)S(1)} %fusion.15), channel_id=1, replica_groups=mesh['dp'=64,'cls'=8] {'cls'}, dimensions={0}, use_global_device_ids=true | all-gather | bytes 589824 | tf_op jit(solution)/shard_map/all_gather | solution.py:70
  185.5 2.7 convolution_bitcast_fusion
  188.1 314.5 %all-reduce.4 = bf16[1568,512]{1,0:T(8,128)(2,1)} all-reduce(f32[1568,512]{1,0:T(8,128)} %convolution_bitcast_fusion), channel_id=1, replica_groups=mesh['dp'=64,'cls'=8] {'dp'}, use_global_device_ids=true, to_apply=%region_7.8 | all-reduce | flops 802816 | bytes 4816896 | tf_op jit(solution)/shard_map/psum | solution.py:74
  502.7 216.9 %all-reduce.3.cloned.1.call-done = f32[512,512]{1,0:T(8,128)} async-done(((f32[512,512]{1,0:T(8,128)}), f32[512,512]{1,0:T(8,128)}) %all-reduce.3.cloned.1.call-update) | async-done | bytes 1048592 | tf_op jit(solution)/shard_map/psum | solution.py:74
  719.5 0.0 copy-start.2
  719.5 1.6 multiply_reduce_fusion
  721.1 0.0 copy-done.2
  721.1 1.1 divide_convert_fusion
  (3 shorter events, 0.0 us)
Async XLA Ops:
  7.2 1.4 copy-start
  7.2 4.9 copy-start.1
  7.2 49.6 %reduce-scatter.3.cloned.1.call-start = ((), (), s32[]{:S(2)}) async-start(), calls=%async_computation.2 | async-start | bytes 589824 | tf_op jit(solution)/shard_map/reduce_scatter | solution.py:32
  11.9 76.8 %copy-start.4 = (s32[512]{0:T(512)S(1)}, s32[512]{0:T(512)}, u32[]{:S(2)}) copy-start(s32[512]{0:T(512)} %param.7) | copy-start | bytes 6148
  12.0 141.3 %reduce-scatter.5.cloned.1.call-start = ((), (), s32[]{:S(2)}) async-start(), calls=%async_computation.3 | async-start | bytes 589824 | tf_op jit(solution)/shard_map/reduce_scatter | solution.py:55
  110.7 42.6 %copy-start.3 = (bf16[64,512]{1,0:T(8,128)(2,1)S(1)}, bf16[64,512]{1,0:T(8,128)(2,1)}, u32[]{:S(2)}) copy-start(bf16[64,512]{1,0:T(8,128)(2,1)} %reduce-scatter.3.cloned.1.call-done) | copy-start | bytes 196612
  110.7 608.9 %all-reduce.3.cloned.1.call-start = ((), (), s32[]{:S(2)}) async-start(), calls=%async_computation.4 | async-start | bytes 2097152 | tf_op jit(solution)/shard_map/psum | solution.py:74
  719.5 1.6 copy-start.2
Sparse Core Ops, SparseCore 0:
  12.1 44.6 reduce-scatter.2
  110.8 42.4 reduce-scatter.4
  156.2 563.3 all-reduce.2
where the time goes:
time: 729 us
  blocking collectives  391 us (54%)
  waiting for transfers between devices  303 us (42%)
  between operations  13.8 us (2%)
  matrix products  10.6 us (1%)
  other arithmetic  8.94 us (1%)
    psum x1, blocking collectives, shards(): fc_total, class_total = lax.psum((fc_part, class_part), 'dp')  315 us
    psum x1, waiting for transfers between devices, shards(): fc_total, class_total = lax.psum((fc_part, class_part), 'dp')  217 us
    reduce_scatter x1, waiting for transfers between devices, shards(): lax.psum_scatter(jnp.dot(rows_block, fc_weight, preferred_element_type=jn...  44.5 us
    reduce_scatter x1, waiting for transfers between devices, shards(): lax.psum_scatter(jnp.dot(rows_block, class_unit, preferred_element_type=j...  41.1 us
    all_gather x1, blocking collectives, shards(): lax.all_gather(raw_grad, 'cls', axis=0, tiled=True)  30.2 us
    all_gather x1, blocking collectives, shards(): faces_all = lax.all_gather(unit_embed, 'cls', axis=0, tiled=True)  30.1 us
    psum x1, blocking collectives, shards(): totals = lax.psum(jnp.sum(powers, axis=1), 'cls')  16.5 us
  transfers between devices with their start and end apart: 3, of which 3 were waited for; matrix products, arithmetic and copies ran while one was open for 1% of the time, Pallas kernels for 0%

commit v1 on v0

--- a/solution.py
+++ b/solution.py
@@ -67,7 +67,9 @@
     rows_block = features
     fc_part = lax.dot_general(
         rows_block,
-        lax.all_gather(raw_grad, "cls", axis=0, tiled=True),
+        jnp.concatenate(
+            lax.all_to_all(jnp.stack([raw_grad] * lax.axis_size("cls")), "cls", 0, 0), axis=0
+        ),
         (((0,), (0,)), ((), ())),
         preferred_element_type=jnp.float32,
     )

time: 729 us -> 1050 us (1.44)
  the two profiles are of different devices: /device:TPU:4 before, /device:TPU:2 now
where the time goes in v1:
time: 1050 us
  waiting for transfers between devices  639 us (61%)
  blocking collectives  365 us (35%)
  between operations  13.8 us (1%)
  matrix products  10.6 us (1%)
    psum x1, waiting for transfers between devices, shards(): fc_total, class_total = lax.psum((fc_part, class_part), 'dp')  553 us
    psum x1, blocking collectives, shards(): fc_total, class_total = lax.psum((fc_part, class_part), 'dp')  317 us
    reduce_scatter x1, waiting for transfers between devices, shards(): lax.psum_scatter(jnp.dot(rows_block, fc_weight, preferred_element_type=jn...  45.8 us
    reduce_scatter x1, waiting for transfers between devices, shards(): lax.psum_scatter(jnp.dot(rows_block, class_unit, preferred_element_type=j...  40.2 us
    all_gather x1, blocking collectives, shards(): faces_all = lax.all_gather(unit_embed, 'cls', axis=0, tiled=True)  30.1 us
  transfers between devices with their start and end apart: 4, of which 3 were waited for; matrix products, arithmetic and copies ran while one was open for 1% of the time, Pallas kernels for 0%

profile of v1, /device:TPU:2, one launch (start us, length us, event | category | flops | bytes accessed | tf_op | source)
XLA Modules:
  0.0 1045.9 jit_solution(8831407258897174986)
XLA Ops:
  7.2 0.0 copy-start
  7.2 0.0 copy-start.1
  7.2 0.0 reduce-scatter.3.cloned.1.call-start
  7.2 1.4 copy-done
  8.6 3.4 convolution_convert_fusion.1
  11.9 0.0 copy-start.4
  11.9 0.0 reduce-scatter.3.cloned.1.call-update
  12.0 0.0 reduce-scatter.5.cloned.1.call-start
  12.0 0.0 copy-done.1
  12.0 0.2 fusion
  12.2 45.8 %reduce-scatter.3.cloned.1.call-done = bf16[64,512]{1,0:T(8,128)(2,1)} async-done(((bf16[512,512]{1,0:T(8,128)(2,1)}), bf16[64,512]{1,0:T(8,128)(2,1)}) %reduce-scatter.3.cloned.1.call-update) | async-done | bytes 65552 | tf_op jit(solution)/shard_map/reduce_scatter | solution.py:32
  58.1 1.0 fusion.12
  59.0 0.9 fusion.16
  60.0 30.1 %all_gather.3 = bf16[512,512]{1,0:T(8,128)(2,1)S(1)} all-gather(bf16[64,512]{1,0:T(8,128)(2,1)S(1)} %fusion.16), channel_id=1, replica_groups=mesh['dp'=64,'cls'=8] {'cls'}, dimensions={0}, use_global_device_ids=true | all-gather | bytes 589824 | tf_op jit(solution)/shard_map/all_gather | solution.py:45
  90.1 0.0 copy-done.4
  90.1 1.9 fusion.8
  91.9 17.3 %psum.21 = f32[512]{0:T(512)S(1)} all-reduce(f32[512]{0:T(512)S(1)} %get-tuple-element.2), channel_id=1, replica_groups=mesh['dp'=64,'cls'=8] {'cls'}, use_global_device_ids=true, to_apply=%region_4.5 | all-reduce | flops 512 | bytes 4096 | tf_op jit(solution)/shard_map/psum | solution.py:52
  109.3 2.2 fusion.6
  111.5 1.3 convolution_convert_fusion
  112.8 0.0 reduce-scatter.5.cloned.1.call-update
  112.8 0.0 copy-start.3
  112.8 0.0 all-reduce.3.cloned.1.call-start
  112.9 1.4 fusion.17
  114.3 0.0 all-reduce.3.cloned.1.call-update
  114.3 40.2 %reduce-scatter.5.cloned.1.call-done = bf16[64,512]{1,0:T(8,128)(2,1)} async-done(((bf16[512,512]{1,0:T(8,128)(2,1)}), bf16[64,512]{1,0:T(8,128)(2,1)}) %reduce-scatter.5.cloned.1.call-update) | async-done | bytes 65552 | tf_op jit(solution)/shard_map/reduce_scatter | solution.py:55
  154.5 0.0 copy-done.3
  154.6 1.0 fusion.13
  155.6 0.9 fusion.15
  156.5 0.9 stack.2
  157.4 6.1 all-to-all-start
  163.5 553.1 %all-reduce.3.cloned.1.call-done = f32[512,512]{1,0:T(8,128)} async-done(((f32[512,512]{1,0:T(8,128)}), f32[512,512]{1,0:T(8,128)}) %all-reduce.3.cloned.1.call-update) | async-done | bytes 1048592 | tf_op jit(solution)/shard_map/psum | solution.py:76
  716.7 0.0 copy-start.2
  716.7 1.6 multiply_reduce_fusion
  718.3 0.0 copy-done.2
  718.3 1.1 divide_convert_fusion
  719.3 0.0 all-to-all-done
  719.3 2.7 convolution_bitcast_fusion
  722.0 317.4 %all-reduce.4 = bf16[1568,512]{1,0:T(8,128)(2,1)} all-reduce(f32[1568,512]{1,0:T(8,128)} %convolution_bitcast_fusion), channel_id=1, replica_groups=mesh['dp'=64,'cls'=8] {'dp'}, use_global_device_ids=true, to_apply=%region_7.8 | all-reduce | flops 802816 | bytes 4816896 | tf_op jit(solution)/shard_map/psum | solution.py:76
  (3 shorter events, 0.0 us)
Async XLA Ops:
  7.2 1.4 copy-start
  7.2 4.9 copy-start.1
  7.2 50.9 %reduce-scatter.3.cloned.1.call-start = ((), (), s32[]{:S(2)}) async-start(), calls=%async_computation.3 | async-start | bytes 589824 | tf_op jit(solution)/shard_map/reduce_scatter | solution.py:32
  11.9 78.1 %copy-start.4 = (s32[512]{0:T(512)S(1)}, s32[512]{0:T(512)}, u32[]{:S(2)}) copy-start(s32[512]{0:T(512)} %param.7) | copy-start | bytes 6148
  12.0 142.6 %reduce-scatter.5.cloned.1.call-start = ((), (), s32[]{:S(2)}) async-start(), calls=%async_computation.4 | async-start | bytes 589824 | tf_op jit(solution)/shard_map/reduce_scatter | solution.py:55
  112.8 41.7 %copy-start.3 = (bf16[64,512]{1,0:T(8,128)(2,1)S(1)}, bf16[64,512]{1,0:T(8,128)(2,1)}, u32[]{:S(2)}) copy-start(bf16[64,512]{1,0:T(8,128)(2,1)} %reduce-scatter.3.cloned.1.call-done) | copy-start | bytes 196612
  112.8 603.8 %all-reduce.3.cloned.1.call-start = ((), (), s32[]{:S(2)}) async-start(), calls=%async_computation.5 | async-start | bytes 2097152 | tf_op jit(solution)/shard_map/psum | solution.py:76
  157.4 561.9 %all-to-all-start = ((bf16[8,64,512]{2,1,0:T(8,128)(2,1)}), bf16[8,64,512]{2,1,0:T(8,128)(2,1)S(1)}, u32[]{:S(2)}, u32[]{:S(2)}) async-start(bf16[8,64,512]{2,1,0:T(8,128)(2,1)} %stack.2), calls=%async_computation.2 | async-start | bytes 1048576 | tf_op jit(solution)/shard_map/all_to_all | solution.py:71
  716.7 1.6 copy-start.2
Sparse Core Ops, SparseCore 0:
  12.1 45.9 reduce-scatter.2
  113.0 41.5 reduce-scatter.4
  158.0 558.5 all-reduce.2
